TPU v7x, 32 devices: a whole 2x2x4 slice. The times are simulated.
32 devices in a mesh: py: 4 (over y, x), px: 8 (over z, core).
Axes of the slice: x: 2, y: 2, z: 4, core: 2. Of those that a mesh axis runs over, the one named last changes fastest.
Arguments:
- movie: bfloat16 [256, 128, 2048], P('py', 'px'), may hold values from -6 to 6
- traces: bfloat16 [4096, 2048], P('py', 'px'), may hold values from -0.125 to 0.125
- footprints: float32 [256, 128, 512], P('py', 'px'), may hold values from 0 to 1
- block_ids: int32 [4, 8, 4], P('py', 'px'), may hold values from 0 to 32, as said below
Outputs:
- updated: float32 [256, 128, 512], P('py', 'px')
Inputs may be any that keep to these rules, and one draw needn't show every extreme that they name: `block_ids`: in each tile's list of 4 entries the live entries come first and are distinct block numbers below 32; the remaining entries equal 32 and mark empty slots. Every tile has at least one live entry, and some tile has all 4 live.
All inputs are finite; a program needn't handle non-finite values.
Results may differ from a plain program's by a relative error of at most 0.0003.
Values may be sent and summed in bfloat16 or wider, within the bound.
A program may use at most 64 MiB of HBM per device.

v0:
```python
import jax
import jax.numpy as jnp
from jax import lax
from jax.sharding import PartitionSpec as P

K = 4096
BLK = 128
SLOTS = 4
ITERS = 2


def accumulate(tile_movie, picked):
    cross = lax.dot_general(
        tile_movie, picked, (((1,), (1,)), ((), ())), preferred_element_type=jnp.float32
    )
    gram = lax.dot_general(
        picked, picked, (((1,), (1,)), ((), ())), preferred_element_type=jnp.float32
    )
    return (cross, gram)


def per_device(movie, traces, footprints, block_ids):
    rows, cols, frames = movie.shape
    pixels = rows * cols
    width = SLOTS * BLK
    nblk = K // BLK
    tile_movie = movie.reshape(pixels, frames)
    ids = block_ids.reshape(SLOTS)
    onehot = (ids[:, None] == jnp.arange(nblk, dtype=jnp.int32)[None, :]).astype(jnp.float32)
    live = jnp.sum(onehot, axis=1)
    span_all = lax.all_gather(traces, "py", axis=0, tiled=True)
    span_len = span_all.shape[1]
    row_ids = lax.all_gather(block_ids, "px", axis=1, tiled=True).reshape(-1, SLOTS)
    route = (row_ids[:, :, None] == jnp.arange(nblk, dtype=jnp.int32)[None, None, :]).astype(
        jnp.bfloat16
    )
    outgoing = jnp.einsum(
        "rsb,bnw->rsnw",
        route,
        span_all.reshape(nblk, BLK, span_len),
        preferred_element_type=jnp.float32,
    )
    outgoing = outgoing.astype(jnp.bfloat16).reshape(row_ids.shape[0], width, span_len)
    received = lax.all_to_all(outgoing, "px", split_axis=0, concat_axis=2, tiled=True)
    mine = received.reshape(width, frames)
    cross, gram = accumulate(tile_movie, mine)
    column_live = jnp.repeat(live, BLK)
    denom = jnp.diagonal(gram) + 1e-06 + (1.0 - column_live)
    current = footprints.reshape(pixels, width) * column_live[None, :]
    pixall = pixels * lax.axis_size("py") * lax.axis_size("px")
    for step in range(ITERS):
        for slot in range(SLOTS):
            low = slot * BLK
            resid = cross[:, low : low + BLK] - jnp.dot(
                current, gram[:, low : low + BLK], precision=lax.Precision.HIGHEST
            )
            fresh = jnp.maximum(
                current[:, low : low + BLK] + resid / denom[None, low : low + BLK], 0.0
            )
            current = current.at[:, low : low + BLK].set(fresh)
        colsq = jnp.sum(current * current, axis=0).reshape(SLOTS, BLK)
        partial_value = jnp.einsum("sb,sn->bn", onehot, colsq, precision=lax.Precision.HIGHEST)
        totals = lax.psum(partial_value, ("py", "px"))
        factor = 1.0 / jnp.sqrt(totals / pixall + 1e-06)
        scale = jnp.einsum("sb,bn->sn", onehot, factor, precision=lax.Precision.HIGHEST).reshape(
            width
        )
        current = current * scale[None, :]
    return current.reshape(rows, cols, width)


def solution(mesh):
    return jax.shard_map(
        per_device,
        mesh=mesh,
        in_specs=(P("py", "px", None), P("py", "px"), P("py", "px", None), P("py", "px", None)),
        out_specs=P("py", "px", None),
        check_vma=False,
    )
```

profile of v0, /device:TPU:0, one launch (start us, length us, event | category | flops | bytes accessed | tf_op | source)
XLA Modules:
  0.0 233.0 jit_solution(12457084238456742489)
XLA Ops:
  6.5 0.0 all-gather.2.cloned.1.call-start
  6.5 0.7 all-gather.2.cloned.1.call-update
  7.3 13.6 %all_gather.6 = s32[1,8,4]{2,0,1:T(1,128)S(1)} all-gather(s32[1,1,4]{2,0,1:T(1,128)} %bitcast.62), channel_id=1, replica_groups=mesh['py'=4,'px'=8] {'px'}, dimensions={1}, use_global_device_ids=true | all-gather | bytes 144 | tf_op jit(solution)/shard_map/all_gather | solution.py:33
  20.9 0.1 copy.48
  21.0 26.1 %all-gather.2.cloned.1.call-done = bf16[4096,256]{1,0:T(8,128)(2,1)} async-done(((bf16[1024,256]{1,0:T(8,128)(2,1)}), bf16[4096,256]{1,0:T(8,128)(2,1)}) %all-gather.2.cloned.1.call-update) | async-done | bytes 2097168 | tf_op jit(solution)/shard_map/all_gather | solution.py:31
  47.1 2.9 %fusion.5 = bf16[8,4,128,256]{3,0,2,1:T(8,128)(2,1)S(1)} fusion(bf16[32,128,256]{2,1,0:T(8,128)(2,1)} %bitcast.60, s32[8,4]{0,1:T(4,128)S(1)} %bitcast.61), kind=kOutput, calls=%fused_computation.8 | convolution fusion | flops 68158464 | bytes 4194432 | tf_op jit(solution)/shard_map/rsb,bnw->rsnw/dot_general | solution.py:37
  50.0 1.7 copy.50
  51.7 0.0 copy-start.3
  51.8 4.7 %all-to-all-start = ((bf16[8,512,256]{2,1,0:T(8,128)(2,1)}), bf16[8,512,256]{2,1,0:T(8,128)(2,1)}, u32[]{:S(2)}, u32[]{:S(2)}) async-start(bf16[8,512,256]{2,1,0:T(8,128)(2,1)} %copy.50), calls=%async_computation | async-start | bytes 4194304 | tf_op jit(solution)/shard_map/all_to_all | solution.py:44
  56.5 0.0 copy-done.3
  56.5 0.0 copy-start.4
  56.5 1.8 copy.46
  58.3 0.6 compare_reduce_fusion.2
  59.0 0.7 compare_reduce_fusion
  59.7 0.0 copy-done.4
  59.7 0.2 convert_reduce_fusion
  59.9 0.1 broadcast_bitcast_fusion
  60.0 1.8 broadcast_multiply_fusion.2
  61.8 43.9 %all-to-all-done = bf16[8,512,256]{2,1,0:T(8,128)(2,1)} async-done(((bf16[8,512,256]{2,1,0:T(8,128)(2,1)}), bf16[8,512,256]{2,1,0:T(8,128)(2,1)}, u32[]{:S(2)}, u32[]{:S(2)}) %all-to-all-start) | async-done | bytes 2097184 | tf_op jit(solution)/shard_map/all_to_all | solution.py:44
  105.6 3.5 %fusion.8 = f32[512,512]{1,0:T(8,128)S(1)} fusion(bf16[8,512,256]{2,1,0:T(8,128)(2,1)} %all-to-all-done), kind=kOutput, calls=%fused_computation.10 | convolution fusion | flops 1073741824 | bytes 3145728 | tf_op jit(solution)/shard_map/dot_general | solution.py:16
  109.1 4.5 %gather_fusion = f32[512]{0:T(512)S(1)} fusion(f32[512,512]{1,0:T(8,128)S(1)} %fusion.8, s32[512]{0:T(512)S(1)} %bitcast.56), kind=kCustom, calls=%fused_computation | custom fusion | bytes 8192 | tf_op jit(solution)/shard_map/jit(diagonal)/cond/branch_0_fun/gather | solution.py:48
  113.7 0.1 subtract_add_fusion
  113.7 3.9 %copy.51 = bf16[1,512,8,256]{1,3,2,0:T(8,128)(2,1)} copy(bf16[1,512,8,256]{3,1,2,0:T(8,128)(2,1)} %bitcast.11) | data formatting | bytes 4194304 | tf_op jit(solution)/shard_map/all_to_all | solution.py:44
  117.7 5.2 %convolution_bitcast_fusion = f32[1024,512]{0,1:T(8,128)S(1)} fusion(bf16[512,2048]{0,1:T(8,128)(2,1)} %bitcast.59, bf16[1024,2048]{1,0:T(8,128)(2,1)} %bitcast.68), kind=kOutput, calls=%fused_computation.9 | convolution fusion | flops 2147483648 | bytes 8388608 | tf_op jit(solution)/shard_map/dot_general | solution.py:13
  122.9 0.0 copy-start.1
  122.9 2.1 fusion.40
  125.0 2.2 fusion.36
  127.2 2.1 fusion.32
  129.3 0.0 copy-done.1
  129.4 1.5 fusion.28
  130.9 0.2 multiply_reduce_fusion.1
  131.1 0.3 fusion.64
  131.3 37.2 %psum.14 = f32[32,128]{1,0:T(8,128)S(1)} all-reduce(f32[32,128]{1,0:T(8,128)S(1)} %fusion.64), channel_id=1, replica_groups=mesh['py'=4,'px'=8] {'py','px'}, use_global_device_ids=true, to_apply=%region_5.6 | all-reduce | flops 4096 | bytes 32768 | tf_op jit(solution)/shard_map/psum | solution.py:63
  168.5 0.2 convolution_bitcast_fusion.2
  168.7 0.0 copy-start.2
  168.7 0.2 broadcast_multiply_fusion.1
  168.9 1.4 copy-done.2
  170.3 2.1 fusion.25
  172.4 2.1 fusion.21
  174.6 2.0 fusion.17
  176.7 1.4 fusion.13
  178.1 0.0 copy-start
  178.2 1.3 copy-done
  179.5 0.2 multiply_reduce_fusion
  179.7 0.3 fusion.62
  179.9 42.4 %psum.15 = f32[32,128]{1,0:T(8,128)S(1)} all-reduce(f32[32,128]{1,0:T(8,128)S(1)} %fusion.62), channel_id=1, replica_groups=mesh['py'=4,'px'=8] {'py','px'}, use_global_device_ids=true, to_apply=%region_7.8 | all-reduce | flops 4096 | bytes 32768 | tf_op jit(solution)/shard_map/psum | solution.py:63
  222.3 0.2 convolution_bitcast_fusion.1
  222.5 1.8 broadcast_multiply_fusion
  224.3 1.8 copy.60
  (10 shorter events, 0.3 us)
Async XLA Ops:
  6.5 40.6 %all-gather.2.cloned.1.call-start = ((), (), s32[]{:S(2)}) async-start(), calls=%async_computation.1 | async-start | bytes 2621440 | tf_op jit(solution)/shard_map/all_gather | solution.py:31
  51.7 4.7 %copy-start.3 = (f32[64,16,512]{2,1,0:T(8,128)S(1)}, f32[64,16,512]{2,1,0:T(8,128)}, u32[]{:S(2)}) copy-start(f32[64,16,512]{2,1,0:T(8,128)} %param.22) | copy-start | bytes 6291460
  51.8 53.9 %all-to-all-start = ((bf16[8,512,256]{2,1,0:T(8,128)(2,1)}), bf16[8,512,256]{2,1,0:T(8,128)(2,1)}, u32[]{:S(2)}, u32[]{:S(2)}) async-start(bf16[8,512,256]{2,1,0:T(8,128)(2,1)} %copy.50), calls=%async_computation | async-start | bytes 4194304 | tf_op jit(solution)/shard_map/all_to_all | solution.py:44
  56.5 3.2 %copy-start.4 = (s32[1,1,4]{2,1,0:T(1,128)S(1)}, s32[1,1,4]{2,1,0:T(1,128)}, u32[]{:S(2)}) copy-start(s32[1,1,4]{2,1,0:T(1,128)} %param.23) | copy-start | bytes 52
  122.9 6.5 %copy-start.1 = (f32[1024,512]{0,1:T(8,128)}, f32[1024,512]{0,1:T(8,128)S(1)}, u32[]{:S(2)}) copy-start(f32[1024,512]{0,1:T(8,128)S(1)} %convolution_bitcast_fusion) | copy-start | bytes 6291460
  168.7 1.6 copy-start.2
  178.1 1.3 copy-start
Sparse Core Ops, SparseCore 0:
  9.2 37.8 all-gather.1
where the time goes:
time: 234 us; the launch traced here: 233 us
  blocking collectives  93.2 us (40%)
  waiting for transfers between devices  70.7 us (30%)
  matrix products  27.9 us (12%)
  local copies, waits for them, and re-layouts  17 us (7%)
  between operations  13.6 us (6%)
  other arithmetic  5.86 us (3%)
  starting transfers between devices  4.74 us (2%)
    psum x2, blocking collectives, per_device(): totals = lax.psum(partial_value, ('py', 'px'))  79.5 us
    all_to_all x1, waiting for transfers between devices, per_device(): lax.all_to_all(outgoing, 'px', split_axis=0, concat_axis=2, tiled=True)  43.9 us
    all_gather x1, waiting for transfers between devices, per_device(): span_all = lax.all_gather(traces, 'py', axis=0, tiled=True)  26.1 us
    dot_general x8, matrix products, per_device(): jnp.dot(current, gram[:, low:low + BLK], precision=lax.Precision.HIGHEST)  15.4 us
    all_gather x1, blocking collectives, per_device(): lax.all_gather(block_ids, 'px', axis=1, tiled=True).reshape(-1, SLOTS)  13.6 us
    dot_general x1, matrix products, accumulate(): lax.dot_general(tile_movie, picked, (((1,), (1,)), ((), ())), preferred_e...  5.2 us
    all_to_all x1, starting transfers between devices, per_device(): lax.all_to_all(outgoing, 'px', split_axis=0, concat_axis=2, tiled=True)  4.74 us
  transfers between devices with their start and end apart: 2, of which 2 were waited for; matrix products, arithmetic and copies ran while one was open for 2% of the time, Pallas kernels for 0%

commit v1 on v0

--- a/solution.py
+++ b/solution.py
@@ -1,3 +1,4 @@
+import functools
 import jax
 import jax.numpy as jnp
 from jax import lax
@@ -7,6 +8,24 @@
 BLK = 128
 SLOTS = 4
 ITERS = 2
+
+
+def handle_regions(field_in, shard_axis):
+    size_here = lax.axis_size(shard_axis)
+    x_new = map(lambda hop_no: (hop_no, (hop_no + 1) % size_here), range(size_here))
+    high = [None] * size_here
+    high[size_here - 1] = field_in
+    tray = list(x_new)
+    for j in range(size_here - 2, -1, -1):
+        high[j] = lax.ppermute(high[j + 1], shard_axis, tray)
+    long_array = jnp.concatenate(high, 0)
+    u_next = jnp.roll(
+        long_array, shift=(lax.axis_index(shard_axis) + 1) * field_in.shape[0], axis=0
+    )
+    return u_next
+
+
+ports_view = functools.partial(handle_regions, shard_axis="py")
 
 
 def accumulate(tile_movie, picked):
@@ -28,7 +47,7 @@
     ids = block_ids.reshape(SLOTS)
     onehot = (ids[:, None] == jnp.arange(nblk, dtype=jnp.int32)[None, :]).astype(jnp.float32)
     live = jnp.sum(onehot, axis=1)
-    span_all = lax.all_gather(traces, "py", axis=0, tiled=True)
+    span_all = ports_view(traces)
     span_len = span_all.shape[1]
     row_ids = lax.all_gather(block_ids, "px", axis=1, tiled=True).reshape(-1, SLOTS)
     route = (row_ids[:, :, None] == jnp.arange(nblk, dtype=jnp.int32)[None, None, :]).astype(

time: 234 us -> 222 us (0.949)
  between operations: 13.6 us -> 0.32 us
  starting transfers between devices: 4.74 us -> 8.34 us
    ppermute x0 -> x3, waiting for transfers between devices: none -> 27.5 us  [handle_regions(): high[j] = lax.ppermute(high[j + 1], shard_axis, tray)]
    all_gather x1 -> x0, waiting for transfers between devices: 26.1 us -> none  [per_device(): span_all = lax.all_gather(traces, 'py', axis=0, tiled=True)]
    ppermute x0 -> x3, starting transfers between devices: none -> 3.69 us  [handle_regions(): high[j] = lax.ppermute(high[j + 1], shard_axis, tray)]
  transfers between devices with their start and end apart: 2 -> 4, of which waited for: 2 -> 4; matrix products, arithmetic and copies ran while one was open for 2% -> 2% of each run, Pallas kernels for 0% -> 0%
where the time goes in v1:
time: 222 us; the launch traced here: 221 us
  blocking collectives  91.7 us (41%)
  waiting for transfers between devices  71.3 us (32%)
  matrix products  26.3 us (12%)
  local copies, waits for them, and re-layouts  17.4 us (8%)
  starting transfers between devices  8.34 us (4%)
  other arithmetic  5.86 us (3%)
    psum x2, blocking collectives, per_device(): totals = lax.psum(partial_value, ('py', 'px'))  79.8 us
    all_to_all x1, waiting for transfers between devices, per_device(): lax.all_to_all(outgoing, 'px', split_axis=0, concat_axis=2, tiled=True)  43.8 us
    ppermute x3, waiting for transfers between devices, handle_regions(): high[j] = lax.ppermute(high[j + 1], shard_axis, tray)  27.5 us
    dot_general x8, matrix products, per_device(): jnp.dot(current, gram[:, low:low + BLK], precision=lax.Precision.HIGHEST)  15.4 us
    all_gather x1, blocking collectives, per_device(): lax.all_gather(block_ids, 'px', axis=1, tiled=True).reshape(-1, SLOTS)  12 us
    dot_general x1, matrix products, accumulate(): lax.dot_general(tile_movie, picked, (((1,), (1,)), ((), ())), preferred_e...  5.2 us
    all_to_all x1, starting transfers between devices, per_device(): lax.all_to_all(outgoing, 'px', split_axis=0, concat_axis=2, tiled=True)  4.65 us
    gather x1, local copies, waits for them, and re-layouts, per_device(): denom = jnp.diagonal(gram) + 1e-06 + (1.0 - column_live)  4.52 us
  transfers between devices with their start and end apart: 4, of which 4 were waited for; matrix products, arithmetic and copies ran while one was open for 2% of the time, Pallas kernels for 0%

profile of v1, /device:TPU:0, one launch (start us, length us, event | category | flops | bytes accessed | tf_op | source)
XLA Modules:
  0.0 221.2 jit_solution(16169197345018727833)
XLA Ops:
  0.0 0.0 copy-start.4
  0.0 3.0 %collective-permute-start = (bf16[1024,256]{1,0:T(8,128)(2,1)}, bf16[1024,256]{1,0:T(8,128)(2,1)S(1)}, u32[]{:S(2)}, u32[]{:S(2)}) collective-permute-start(bf16[1024,256]{1,0:T(8,128)(2,1)} %param.21), channel_id=1, source_target_pairs={{0,8},{8,16},{16,24},{24,0},{1,9},{9,17},{17,25},{25,1},{2,10},{10... | collective-permute-start | bytes 1572872 | tf_op jit(solution)/shard_map/ppermute | solution.py:20
  3.0 13.2 %collective-permute-done = bf16[1024,256]{1,0:T(8,128)(2,1)S(1)} collective-permute-done((bf16[1024,256]{1,0:T(8,128)(2,1)}, bf16[1024,256]{1,0:T(8,128)(2,1)S(1)}, u32[]{:S(2)}, u32[]{:S(2)}) %collective-permute-start) | collective-permute-done | bytes 524320 | tf_op jit(solution)/shard_map/ppermute | solution.py:20
  16.1 0.7 collective-permute-start.1
  16.8 13.3 %collective-permute-done.1 = bf16[1024,256]{1,0:T(8,128)(2,1)S(1)} collective-permute-done((bf16[1024,256]{1,0:T(8,128)(2,1)S(1)}, bf16[1024,256]{1,0:T(8,128)(2,1)S(1)}, u32[]{:S(2)}, u32[]{:S(2)}) %collective-permute-start.1) | collective-permute-done | bytes 524320 | tf_op jit(solution)/shard_map/ppermute | solution.py:20
  30.1 0.0 collective-permute-start.2
  30.1 12.0 %all_gather.3 = s32[1,8,4]{2,0,1:T(1,128)S(1)} all-gather(s32[1,1,4]{2,0,1:T(1,128)} %bitcast.62), channel_id=1, replica_groups=mesh['py'=4,'px'=8] {'px'}, dimensions={1}, use_global_device_ids=true | all-gather | bytes 144 | tf_op jit(solution)/shard_map/all_gather | solution.py:52
  42.1 0.1 copy.48
  42.2 1.1 collective-permute-done.2
  43.4 0.0 copy-done.4
  43.6 0.1 constant_dynamic-slice_fusion
  43.8 1.3 fusion.5
  45.1 1.7 copy.50
  46.8 0.0 copy-start.3
  46.8 4.7 %all-to-all-start = ((bf16[8,512,256]{2,1,0:T(8,128)(2,1)}), bf16[8,512,256]{2,1,0:T(8,128)(2,1)}, u32[]{:S(2)}, u32[]{:S(2)}) async-start(bf16[8,512,256]{2,1,0:T(8,128)(2,1)} %copy.50), calls=%async_computation | async-start | bytes 4194304 | tf_op jit(solution)/shard_map/all_to_all | solution.py:63
  51.5 0.0 copy-done.3
  51.5 0.0 copy-start.5
  51.5 1.8 copy.46
  53.3 0.6 compare_reduce_fusion.2
  54.0 0.7 compare_reduce_fusion
  54.7 0.0 copy-done.5
  54.7 0.2 convert_reduce_fusion
  54.9 0.1 broadcast_bitcast_fusion
  54.9 1.8 broadcast_multiply_fusion.2
  56.7 43.8 %all-to-all-done = bf16[8,512,256]{2,1,0:T(8,128)(2,1)} async-done(((bf16[8,512,256]{2,1,0:T(8,128)(2,1)}), bf16[8,512,256]{2,1,0:T(8,128)(2,1)}, u32[]{:S(2)}, u32[]{:S(2)}) %all-to-all-start) | async-done | bytes 2097184 | tf_op jit(solution)/shard_map/all_to_all | solution.py:63
  100.5 3.9 %copy.51 = bf16[1,512,8,256]{1,3,2,0:T(8,128)(2,1)} copy(bf16[1,512,8,256]{3,1,2,0:T(8,128)(2,1)} %bitcast.11) | data formatting | bytes 4194304 | tf_op jit(solution)/shard_map/all_to_all | solution.py:63
  104.4 3.5 %fusion.8 = f32[512,512]{1,0:T(8,128)S(1)} fusion(bf16[8,512,256]{2,1,0:T(8,128)(2,1)} %all-to-all-done), kind=kOutput, calls=%fused_computation.10 | convolution fusion | flops 1073741824 | bytes 3145728 | tf_op jit(solution)/shard_map/dot_general | solution.py:35
  107.9 4.5 %gather_fusion = f32[512]{0:T(512)S(1)} fusion(f32[512,512]{1,0:T(8,128)S(1)} %fusion.8, s32[512]{0:T(512)S(1)} %bitcast.56), kind=kCustom, calls=%fused_computation | custom fusion | bytes 8192 | tf_op jit(solution)/shard_map/jit(diagonal)/cond/branch_0_fun/gather | solution.py:67
  112.5 0.1 subtract_add_fusion
  112.6 5.2 %convolution_bitcast_fusion = f32[1024,512]{0,1:T(8,128)S(1)} fusion(bf16[512,2048]{0,1:T(8,128)(2,1)} %bitcast.60, bf16[1024,2048]{1,0:T(8,128)(2,1)} %bitcast.68), kind=kOutput, calls=%fused_computation.9 | convolution fusion | flops 2147483648 | bytes 8388608 | tf_op jit(solution)/shard_map/dot_general | solution.py:32
  117.8 0.0 copy-start.1
  117.8 2.1 fusion.40
  119.9 2.1 fusion.36
  122.1 2.1 fusion.32
  124.2 0.0 copy-done.1
  124.2 1.5 fusion.28
  125.7 0.2 multiply_reduce_fusion.1
  125.9 0.3 fusion.64
  126.2 37.4 %psum.14 = f32[32,128]{1,0:T(8,128)S(1)} all-reduce(f32[32,128]{1,0:T(8,128)S(1)} %fusion.64), channel_id=1, replica_groups=mesh['py'=4,'px'=8] {'py','px'}, use_global_device_ids=true, to_apply=%region_5.6 | all-reduce | flops 4096 | bytes 32768 | tf_op jit(solution)/shard_map/psum | solution.py:82
  163.5 0.2 convolution_bitcast_fusion.2
  163.7 0.0 copy-start.2
  163.7 0.2 broadcast_multiply_fusion.1
  163.9 1.4 copy-done.2
  165.3 2.1 fusion.25
  167.4 2.1 fusion.21
  169.6 2.0 fusion.17
  171.7 1.4 fusion.13
  173.2 0.0 copy-start
  173.2 1.3 copy-done
  174.5 0.2 multiply_reduce_fusion
  174.7 0.3 fusion.62
  175.0 42.4 %psum.15 = f32[32,128]{1,0:T(8,128)S(1)} all-reduce(f32[32,128]{1,0:T(8,128)S(1)} %fusion.62), channel_id=1, replica_groups=mesh['py'=4,'px'=8] {'py','px'}, use_global_device_ids=true, to_apply=%region_7.8 | all-reduce | flops 4096 | bytes 32768 | tf_op jit(solution)/shard_map/psum | solution.py:82
  217.4 0.2 convolution_bitcast_fusion.1
  217.6 1.8 broadcast_multiply_fusion
  219.4 1.8 copy.60
  (18 shorter events, 0.6 us)
Async XLA Ops:
  0.0 43.4 %copy-start.4 = (bf16[1024,256]{1,0:T(8,128)(2,1)S(1)}, bf16[1024,256]{1,0:T(8,128)(2,1)}, u32[]{:S(2)}) copy-start(bf16[1024,256]{1,0:T(8,128)(2,1)} %param.21) | copy-start | bytes 1572868
  0.0 16.1 %collective-permute-start = (bf16[1024,256]{1,0:T(8,128)(2,1)}, bf16[1024,256]{1,0:T(8,128)(2,1)S(1)}, u32[]{:S(2)}, u32[]{:S(2)}) collective-permute-start(bf16[1024,256]{1,0:T(8,128)(2,1)} %param.21), channel_id=1, source_target_pairs={{0,8},{8,16},{16,24},{24,0},{1,9},{9,17},{17,25},{25,1},{2,10},{10... | collective-permute-start | bytes 1572872 | tf_op jit(solution)/shard_map/ppermute | solution.py:20
  16.1 14.0 %collective-permute-start.1 = (bf16[1024,256]{1,0:T(8,128)(2,1)S(1)}, bf16[1024,256]{1,0:T(8,128)(2,1)S(1)}, u32[]{:S(2)}, u32[]{:S(2)}) collective-permute-start(bf16[1024,256]{1,0:T(8,128)(2,1)S(1)} %collective-permute-done), channel_id=1, source_target_pairs={{0,8},{8,16},{16,24},{24,0},{1,9},{9,17},{17,25},{25,1},{2,10},{10... | collective-permute-start | bytes 1572872 | tf_op jit(solution)/shard_map/ppermute | solution.py:20
  30.1 13.1 %collective-permute-start.2 = (bf16[1024,256]{1,0:T(8,128)(2,1)S(1)}, bf16[1024,256]{1,0:T(8,128)(2,1)S(1)}, u32[]{:S(2)}, u32[]{:S(2)}) collective-permute-start(bf16[1024,256]{1,0:T(8,128)(2,1)S(1)} %collective-permute-done.1), channel_id=1, source_target_pairs={{0,8},{8,16},{16,24},{24,0},{1,9},{9,17},{17,25},{25,1},{2,10},{10... | collective-permute-start | bytes 1572872 | tf_op jit(solution)/shard_map/ppermute | solution.py:20
  46.8 4.7 %copy-start.3 = (f32[64,16,512]{2,1,0:T(8,128)S(1)}, f32[64,16,512]{2,1,0:T(8,128)}, u32[]{:S(2)}) copy-start(f32[64,16,512]{2,1,0:T(8,128)} %param.22) | copy-start | bytes 6291460
  46.8 53.7 %all-to-all-start = ((bf16[8,512,256]{2,1,0:T(8,128)(2,1)}), bf16[8,512,256]{2,1,0:T(8,128)(2,1)}, u32[]{:S(2)}, u32[]{:S(2)}) async-start(bf16[8,512,256]{2,1,0:T(8,128)(2,1)} %copy.50), calls=%async_computation | async-start | bytes 4194304 | tf_op jit(solution)/shard_map/all_to_all | solution.py:63
  51.5 3.2 %copy-start.5 = (s32[1,1,4]{2,1,0:T(1,128)S(1)}, s32[1,1,4]{2,1,0:T(1,128)}, u32[]{:S(2)}) copy-start(s32[1,1,4]{2,1,0:T(1,128)} %param.23) | copy-start | bytes 52
  117.8 6.4 %copy-start.1 = (f32[1024,512]{0,1:T(8,128)}, f32[1024,512]{0,1:T(8,128)S(1)}, u32[]{:S(2)}) copy-start(f32[1024,512]{0,1:T(8,128)S(1)} %convolution_bitcast_fusion) | copy-start | bytes 6291460
  163.7 1.6 copy-start.2
  173.2 1.3 copy-start
